TPU v7x, 32 devices: a whole 2x2x4 slice. The times are simulated.
32 devices in a mesh: ves: 16 (over z, y, x), sec: 2 (over core).
Axes of the slice: x: 2, y: 2, z: 4, core: 2. Of those that a mesh axis runs over, the one named last changes fastest.
Arguments:
- density: bfloat16 [8192, 3, 544], P(('ves', 'sec')), may hold values from -6 to 6
- analysis: bfloat16 [544, 289], replicated, may hold values from -0.25 to 0.25
- synthesis: bfloat16 [289, 544], replicated, may hold values from -0.375 to 0.375
- degree_gain: float32 [289], replicated, may hold values from 0.05 to 2
- near_kernel: bfloat16 [544, 544], replicated, may hold values from -0.25 to 0.25
- partners: int32 [8192, 4], P(('ves', 'sec')), may hold values from 0 to 8191, as said below
- pair_weight: float32 [8192, 4], P(('ves', 'sec')), may hold values from 0.2 to 1
- wall_list: int32 [512], P(('ves', 'sec')), may hold values from 0 to 8191, as said below
- coupling: bfloat16 [4096, 32], P(('ves', 'sec')), may hold values from -1 to 1
- wall_gain: float32 [4096], P(('ves', 'sec')), may hold values from 0.5 to 2
Outputs:
- velocity: float32 [8192, 3, 544], P(('ves', 'sec'))
Inputs may be any that keep to these rules, and one draw needn't show every extreme that they name: `partners`: vesicles form blocks of 256 consecutive ids, block b in region b // 2, slot b % 2. A partner of vesicle i lies in the block of i, or among the last 64 vesicles of the block of the region below with the same slot, or among the first 64 of the block of the region above with the same slot. No vesicle is its own partner. `wall_list`: entry block b (entries b * 16 to b * 16 + 15) holds 16 distinct ids of vesicle block b.
All inputs are finite; a program needn't handle non-finite values.
Results may differ from a plain program's by a relative error of at most 0.0043.
Values may be sent and summed in bfloat16 or wider, within the bound.
A program may use at most 64 MiB of HBM per device.

v0:
```python
import jax
import jax.numpy as jnp
from jax import lax
from jax.sharding import PartitionSpec as P


def with_halo(cells, sides, width):
    for axis, dim in sides:
        count = lax.axis_size(axis)
        ends = count - 1
        head = lax.slice_in_dim(cells, 0, width, axis=dim)
        tail = lax.slice_in_dim(cells, cells.shape[dim] - width, cells.shape[dim], axis=dim)
        cells = jnp.concatenate(
            [
                lax.ppermute(tail, axis, [(i, (i + 1) % count) for i in range(ends)]),
                cells,
                lax.ppermute(head, axis, [((i + 1) % count, i) for i in range(ends)]),
            ],
            axis=dim,
        )
    return cells


def shards(
    density,
    analysis,
    synthesis,
    degree_gain,
    near_kernel,
    partners,
    pair_weight,
    wall_list,
    coupling,
    wall_gain,
):
    count = density.shape[0]
    num_points = density.shape[2]
    num_coefs = analysis.shape[1]
    edge = count // 4
    coef = jnp.dot(
        density.reshape(count * 3, num_points), analysis, preferred_element_type=jnp.float32
    ).astype(jnp.bfloat16)
    smooth = jnp.dot(coef, synthesis, preferred_element_type=jnp.float32).astype(jnp.bfloat16)
    scaled = (coef.astype(jnp.float32) * degree_gain).astype(jnp.bfloat16)
    self_vel = jnp.dot(scaled, synthesis, preferred_element_type=jnp.float32)
    smooth = smooth.reshape(count, 3, num_points)
    window = with_halo(smooth, (("ves", 0),), edge)
    target = partners // count
    inner = partners % count
    region_now = lax.axis_index("ves")
    shift = target // lax.axis_size("sec") - region_now
    slot_index = inner + edge + shift * count
    gathered = jnp.take(window, slot_index.reshape(-1), axis=0).reshape(
        count, partners.shape[1], 3, num_points
    )
    mixed = jnp.zeros((count, 3, num_points), jnp.float32)
    for k in range(partners.shape[1]):
        mixed = mixed + pair_weight[:, k, None, None] * gathered[:, k].astype(jnp.float32)
    mixed = mixed.astype(jnp.bfloat16).reshape(count * 3, num_points)
    near_vel = jnp.dot(mixed, near_kernel, preferred_element_type=jnp.float32)
    near_wall = wall_list.shape[0]
    local_ids = wall_list % count
    picked = jnp.take(coef.reshape(count, 3 * num_coefs), local_ids, axis=0)
    region_coefs = lax.all_gather(picked, "sec", axis=0, tiled=True)
    all_coupling, all_gain = (
        lax.all_gather(coupling.astype(jnp.float32), "sec", axis=0, tiled=True),
        lax.all_gather(wall_gain, "sec", axis=0, tiled=True),
    )
    all_coupling = all_coupling.astype(jnp.bfloat16)
    all_dens = (
        all_gain[:, None] * jnp.dot(all_coupling, region_coefs, preferred_element_type=jnp.float32)
    ).astype(jnp.bfloat16)
    own_columns = lax.dynamic_slice_in_dim(
        all_coupling, lax.axis_index("sec") * near_wall, near_wall, 1
    )
    back = lax.dot_general(
        own_columns, all_dens, (((0,), (0,)), ((), ())), preferred_element_type=jnp.float32
    )
    wall_coef = back.astype(jnp.bfloat16).reshape(near_wall * 3, num_coefs)
    wall_points = jnp.dot(wall_coef, synthesis, preferred_element_type=jnp.float32).reshape(
        near_wall, 3 * num_points
    )
    placing = (local_ids[:, None] == jnp.arange(count, dtype=jnp.int32)[None, :]).astype(
        jnp.float32
    )
    wall_vel = lax.dot_general(
        placing,
        wall_points,
        (((0,), (0,)), ((), ())),
        precision=lax.Precision.HIGHEST,
        preferred_element_type=jnp.float32,
    )
    velocity = (
        self_vel.reshape(count, 3, num_points)
        + near_vel.reshape(count, 3, num_points)
        + wall_vel.reshape(count, 3, num_points)
    )
    return velocity


def solution(mesh):
    return jax.shard_map(
        shards,
        mesh=mesh,
        in_specs=(
            P(("ves", "sec"), None, None),
            P(),
            P(),
            P(),
            P(),
            P(("ves", "sec"), None),
            P(("ves", "sec"), None),
            P(("ves", "sec")),
            P(("ves", "sec"), None),
            P(("ves", "sec")),
        ),
        out_specs=P(("ves", "sec"), None, None),
        check_vma=False,
    )
```

profile of v0, /device:TPU:25, one launch (start us, length us, event | category | flops | bytes accessed | tf_op | source)
XLA Modules:
  0.0 66.1 jit_solution(10331500423084310417)
XLA Ops:
  0.0 2.7 %copy.115 = bf16[256,3,544]{2,1,0:T(4,128)(2,1)S(1)} copy(bf16[256,3,544]{0,2,1:T(8,128)(2,1)} %param.10) | data formatting | bytes 1671168 | tf_op args[0]
  2.7 1.6 %reshape.117 = bf16[768,544]{1,0:T(8,128)(2,1)} reshape(bf16[256,3,544]{2,1,0:T(4,128)(2,1)S(1)} %copy.115) | data formatting | bytes 1671168 | tf_op jit(solution)/shard_map/reshape | solution.py:41
  4.4 1.8 %convolution_convert_fusion.1 = bf16[768,289]{0,1:T(8,128)(2,1)S(1)} fusion(bf16[768,544]{1,0:T(8,128)(2,1)} %reshape.117, bf16[544,289]{0,1:T(8,128)(2,1)S(1)} %copy-done.7), kind=kOutput, calls=%fused_computation.15 | convolution fusion | flops 241705728 | bytes 1593920 | tf_op jit(solution)/shard_map/dot_general | solution.py:40
  6.1 0.7 convolution_convert_fusion
  6.8 0.1 fusion.32
  7.0 0.2 copy.117
  7.1 0.9 %slice.38 = bf16[64,3,544]{2,1,0:T(4,128)(2,1)} reshape(bf16[192,544]{1,0:T(8,128)(2,1)S(1)} %copy.117) | data formatting | bytes 417792 | tf_op jit(solution)/shard_map/slice | solution.py:12
  8.0 3.1 %collective-permute-start = (bf16[64,3,544]{2,1,0:T(4,128)(2,1)}, bf16[64,3,544]{2,1,0:T(4,128)(2,1)}, u32[]{:S(2)}, u32[]{:S(2)}) collective-permute-start(bf16[64,3,544]{2,1,0:T(4,128)(2,1)} %slice.38), channel_id=1, source_target_pairs={{0,2},{2,4},{4,6},{6,8},{8,10},{10,12},{12,14},{14,16},{16,18},{18... | collective-permute-start | bytes 626696 | tf_op jit(solution)/shard_map/ppermute | solution.py:15
  11.1 0.2 copy.119
  11.3 0.9 %slice.40 = bf16[64,3,544]{2,1,0:T(4,128)(2,1)} reshape(bf16[192,544]{1,0:T(8,128)(2,1)S(1)} %copy.119) | data formatting | bytes 417792 | tf_op jit(solution)/shard_map/slice | solution.py:11
  12.2 3.9 %collective-permute-start.1 = (bf16[64,3,544]{2,1,0:T(4,128)(2,1)}, bf16[64,3,544]{2,1,0:T(4,128)(2,1)}, u32[]{:S(2)}, u32[]{:S(2)}) collective-permute-start(bf16[64,3,544]{2,1,0:T(4,128)(2,1)} %slice.40), channel_id=1, source_target_pairs={{2,0},{4,2},{6,4},{8,6},{10,8},{12,10},{14,12},{16,14},{18,16},{20... | collective-permute-start | bytes 626696 | tf_op jit(solution)/shard_map/ppermute | solution.py:17
  16.1 0.6 copy.118
  16.8 0.3 copy.125
  17.1 1.3 %reshape.119 = bf16[256,3,544]{2,1,0:T(4,128)(2,1)} reshape(bf16[768,544]{1,0:T(8,128)(2,1)S(1)} %copy.118) | data formatting | bytes 1671168 | tf_op jit(solution)/shard_map/reshape | solution.py:46
  18.5 0.1 copy.120
  18.8 0.5 reshape.121
  19.3 0.6 gather_fusion.1
  20.0 2.7 %all_gather.11 = bf16[32,867]{1,0:T(8,128)(2,1)S(1)} all-gather(bf16[16,867]{1,0:T(8,128)(2,1)S(1)} %broadcast_select_fusion.1), channel_id=1, replica_groups=mesh['ves'=16,'sec'=2] {'sec'}, dimensions={0}, use_global_device_ids=true | all-gather | bytes 83232 | tf_op jit(solution)/shard_map/all_gather | solution.py:64
  22.8 1.8 %all_gather.9 = bf16[256,32]{0,1:T(8,128)(2,1)S(1)} all-gather(bf16[128,32]{0,1:T(8,128)(2,1)S(1)} %copy-done.3), channel_id=1, replica_groups=mesh['ves'=16,'sec'=2] {'sec'}, dimensions={0}, use_global_device_ids=true | all-gather | bytes 24576 | tf_op jit(solution)/shard_map/all_gather | solution.py:66
  24.6 2.0 %all-gather = f32[2,1,128]{2,1,0:T(1,128)S(1)} all-gather(f32[1,1,128]{2,1,0:T(1,128)S(1)} %bitcast.57), channel_id=1, replica_groups=mesh['ves'=16,'sec'=2] {'sec'}, dimensions={0}, use_global_device_ids=true | all-gather | bytes 1536 | tf_op jit(solution)/shard_map/all_gather | solution.py:67
  26.6 0.5 fusion.6
  27.2 0.2 fusion.34
  27.7 2.2 %fusion.14 = f32[768,544]{1,0:T(8,128)} fusion(bf16[289,544]{1,0:T(8,128)(2,1)S(1)} %copy-done.2, bf16[768,289]{0,1:T(8,128)(2,1)S(1)} %convolution_convert_fusion.1, f32[289]{0:T(512)S(1)} %copy-done.6), kind=kOutput, calls=%fused_computation.30 | convolution fusion | flops 242149632 | bytes 2430660 | tf_op jit(solution)/shard_map/dot_general | solution.py:45
  29.9 2.8 %reshape.118 = f32[256,3,544]{2,1,0:T(4,128)S(1)} reshape(f32[768,544]{1,0:T(8,128)} %fusion.14) | data formatting | bytes 3342336 | tf_op jit(solution)/shard_map/reshape | solution.py:94
  32.7 2.3 %copy.124 = f32[256,3,544]{0,2,1:T(8,128)} copy(f32[256,3,544]{2,1,0:T(4,128)S(1)} %reshape.118) | data formatting | bytes 3342336 | tf_op jit(solution)/shard_map/reshape | solution.py:94
  35.0 4.3 %pad_maximum_fusion = bf16[384,3,544]{2,1,0:T(4,128)(2,1)S(1)} fusion(bf16[64,3,544]{2,1,0:T(4,128)(2,1)} %collective-permute-done.1, bf16[256,3,544]{2,1,0:T(4,128)(2,1)} %reshape.119, bf16[64,3,544]{2,1,0:T(4,128)(2,1)} %collective-permute-done), kind=kLoop, calls=%fused_computation.3 | loop fusion | flops 1253376 | bytes 2506752 | tf_op jit(solution)/shard_map/concatenate | solution.py:13
  39.3 12.3 %gather_fusion = bf16[1024,3,544]{2,1,0:T(4,128)(2,1)} fusion(bf16[384,3,544]{2,1,0:T(4,128)(2,1)S(1)} %pad_maximum_fusion, s32[1024]{0:T(1024)S(1)} %broadcast_clamp_fusion), kind=kCustom, calls=%fused_computation | custom fusion | bytes 6688768 | tf_op jit(solution)/shard_map/jit(_take)/gather | solution.py:53
  51.6 8.7 %copy.122 = bf16[256,4,3,544]{0,3,2,1:T(8,128)(2,1)} copy(bf16[256,4,3,544]{3,2,1,0:T(4,128)(2,1)} %bitcast.50) | data formatting | bytes 6684672 | tf_op jit(solution)/shard_map/jit(_take)/gather | solution.py:53
  60.3 2.3 %broadcast_select_fusion = bf16[256,4,3,544]{0,3,2,1:T(8,128)(2,1)S(1)} fusion(bf16[256,4,3,544]{0,3,2,1:T(8,128)(2,1)} %copy.122, pred[256,4]{0,1:T(4,128)(4,1)S(1)} %get-tuple-element.7), kind=kLoop, calls=%fused_computation.2 | loop fusion | flops 1671168 | bytes 6685696 | tf_op jit(solution)/shard_map/jit(_take)/select_n | solution.py:53
  62.6 1.2 %fusion.7 = f32[256,3,544]{0,2,1:T(8,128)S(1)} fusion(bf16[256,4,3,544]{0,3,2,1:T(8,128)(2,1)S(1)} %broadcast_select_fusion, f32[256]{0:T(256)S(1)} %bitcast.55, f32[256]{0:T(256)S(1)} %bitcast.56, f32[256]{0:T(256)S(1)} %bitcast.54, f32[256]{0:T(256)S(1)} %bitcast.53, bf16[544,544]{1,0:T(8,128)(2,1)S(1)} %copy-done), kind=kOutput, calls=%fused_computation.20 | convolution fusion | flops 459571200 | bytes 5609472 | tf_op jit(solution)/shard_map/dot_general | solution.py:60
  63.8 0.2 copy-done.1
  64.0 2.1 %add_add_fusion = f32[256,3,544]{0,2,1:T(8,128)} fusion(f32[256,3,544]{0,2,1:T(8,128)S(1)} %copy-done.1, f32[256,3,544]{0,2,1:T(8,128)S(1)} %fusion.7, f32[3,544,16]{1,0,2:T(4,128)S(1)} %dot_general.36, s32[16]{0:T(128)S(1)} %get-tuple-element.6), kind=kOutput, calls=%fused_computation.12 | convolution fusion | flops 81055744 | bytes 5118016 | tf_op jit(solution)/shard_map/dot_general | solution.py:86
  (33 shorter events, 0.7 us)
Async XLA Ops:
  0.0 62.5 %copy-start = (bf16[544,544]{1,0:T(8,128)(2,1)S(1)}, bf16[544,544]{1,0:T(8,128)(2,1)}, u32[]{:S(2)}) copy-start(bf16[544,544]{1,0:T(8,128)(2,1)} %param.14) | copy-start | bytes 1775620
  2.7 1.7 %copy-start.7 = (bf16[544,289]{0,1:T(8,128)(2,1)S(1)}, bf16[544,289]{0,1:T(8,128)(2,1)}, u32[]{:S(2)}) copy-start(bf16[544,289]{0,1:T(8,128)(2,1)} %param.11) | copy-start | bytes 943300
  2.7 3.4 %copy-start.2 = (bf16[289,544]{1,0:T(8,128)(2,1)S(1)}, bf16[289,544]{1,0:T(8,128)(2,1)}, u32[]{:S(2)}) copy-start(bf16[289,544]{1,0:T(8,128)(2,1)} %param.12) | copy-start | bytes 943300
  8.0 27.0 %collective-permute-start = (bf16[64,3,544]{2,1,0:T(4,128)(2,1)}, bf16[64,3,544]{2,1,0:T(4,128)(2,1)}, u32[]{:S(2)}, u32[]{:S(2)}) collective-permute-start(bf16[64,3,544]{2,1,0:T(4,128)(2,1)} %slice.38), channel_id=1, source_target_pairs={{0,2},{2,4},{4,6},{6,8},{8,10},{10,12},{12,14},{14,16},{16,18},{18... | collective-permute-start | bytes 626696 | tf_op jit(solution)/shard_map/ppermute | solution.py:15
  12.2 22.8 %collective-permute-start.1 = (bf16[64,3,544]{2,1,0:T(4,128)(2,1)}, bf16[64,3,544]{2,1,0:T(4,128)(2,1)}, u32[]{:S(2)}, u32[]{:S(2)}) collective-permute-start(bf16[64,3,544]{2,1,0:T(4,128)(2,1)} %slice.40), channel_id=1, source_target_pairs={{2,0},{4,2},{6,4},{8,6},{10,8},{12,10},{14,12},{16,14},{18,16},{20... | collective-permute-start | bytes 626696 | tf_op jit(solution)/shard_map/ppermute | solution.py:17
  16.8 1.7 %copy-start.4 = (s32[256,4]{0,1:T(4,128)S(1)}, s32[256,4]{0,1:T(4,128)}, u32[]{:S(2)}) copy-start(s32[256,4]{0,1:T(4,128)} %param.15) | copy-start | bytes 12292
  17.1 2.2 %copy-start.8 = (s32[16]{0:T(128)S(1)}, s32[16]{0:T(128)}, u32[]{:S(2)}) copy-start(s32[16]{0:T(128)} %param.17) | copy-start | bytes 196
  17.1 5.7 %copy-start.3 = (bf16[128,32]{0,1:T(8,128)(2,1)S(1)}, bf16[128,32]{0,1:T(8,128)(2,1)}, u32[]{:S(2)}) copy-start(bf16[128,32]{0,1:T(8,128)(2,1)} %param.18) | copy-start | bytes 24580
  17.1 7.5 %copy-start.9 = (f32[128]{0:T(128)S(1)}, f32[128]{0:T(128)}, u32[]{:S(2)}) copy-start(f32[128]{0:T(128)} %param.19) | copy-start | bytes 1540
  18.5 9.2 %copy-start.6 = (f32[289]{0:T(512)S(1)}, f32[289]{0:T(512)}, u32[]{:S(2)}) copy-start(f32[289]{0:T(512)} %param.13) | copy-start | bytes 3472
  32.7 2.3 %copy-start.5 = (f32[256,4]{0,1:T(4,128)S(1)}, f32[256,4]{0,1:T(4,128)}, u32[]{:S(2)}) copy-start(f32[256,4]{0,1:T(4,128)} %param.16) | copy-start | bytes 12292
  62.6 1.4 %copy-start.1 = (f32[256,3,544]{0,2,1:T(8,128)S(1)}, f32[256,3,544]{0,2,1:T(8,128)}, u32[]{:S(2)}) copy-start(f32[256,3,544]{0,2,1:T(8,128)} %copy.124) | copy-start | bytes 5013508
where the time goes:
time: 66.7 us; the launch traced here: 66.1 us
  local copies, waits for them, and re-layouts  36.9 us (55%)
  matrix products  8.65 us (13%)
  starting transfers between devices  7.06 us (11%)
  other arithmetic  6.69 us (10%)
  blocking collectives  6.54 us (10%)
    gather x2, local copies, waits for them, and re-layouts, shards(): jnp.take(window, slot_index.reshape(-1), axis=0)  21 us
    reshape x2, local copies, waits for them, and re-layouts, shards(): self_vel.reshape(count, 3, num_points)  5.08 us
    concatenate x1, other arithmetic, with_halo(): jnp.concatenate([lax.ppermute(tail, axis, [(i, (i + 1) % count) for i in...  4.29 us
    ppermute x1, starting transfers between devices, with_halo(): lax.ppermute(head, axis, [((i + 1) % count, i) for i in range(ends)])  3.94 us
    ppermute x1, starting transfers between devices, with_halo(): lax.ppermute(tail, axis, [(i, (i + 1) % count) for i in range(ends)])  3.11 us
    unnamed x21, local copies, waits for them, and re-layouts  2.97 us
    all_gather x1, blocking collectives, shards(): region_coefs = lax.all_gather(picked, 'sec', axis=0, tiled=True)  2.72 us
    select_n x2, other arithmetic, shards(): jnp.take(window, slot_index.reshape(-1), axis=0)  2.26 us
  transfers between devices with their start and end apart: 2, of which 0 were waited for; matrix products, arithmetic and copies ran while one was open for 20% of the time, Pallas kernels for 0%

commit v1 on v0

v1 whole, which is shorter than its diff:
```python
import functools

import jax
import jax.numpy as jnp
from jax import lax
from jax.experimental import pallas as pl
from jax.experimental.pallas import tpu as pltpu
from jax.sharding import PartitionSpec as P

MESH = pl.DeviceIdType.MESH
F32 = jnp.float32
BF16 = jnp.bfloat16


def dot(a, b, ca=1, cb=0):
    return lax.dot_general(a, b, (((ca,), (cb,)), ((), ())), preferred_element_type=F32)


def step_kernel(
    n_ves,
    n_sec,
    dens_ref,
    ana_ref,
    syn_ref,
    gain_ref,
    near_ref,
    part_ref,
    weight_ref,
    list_ref,
    coup_ref,
    wgain_ref,
    out_ref,
    coef_ref,
    mix_ref,
    tail01,
    tail2,
    head01,
    head2,
    recv01,
    recv2,
    halo2,
    pick_all,
    coup_all,
    gain_all,
    send_sem,
    recv_sem,
    wall_send,
    wall_recv,
):
    ves = lax.axis_index("ves")
    sec = lax.axis_index("sec")
    comps, num_points, count = dens_ref.shape
    num_coefs = ana_ref.shape[0]
    near_wall = list_ref.shape[0]
    edge = count // 4
    tile = 2 * edge
    cut = recv2.shape[1]
    top = num_coefs - cut
    has_left = ves > 0
    has_right = ves < n_ves - 1
    hops = range(1, n_sec)

    barrier = pltpu.get_barrier_semaphore()

    @pl.when(has_left)
    def _():
        pl.semaphore_signal(barrier, inc=1, device_id=(ves - 1, sec), device_id_type=MESH)

    @pl.when(has_right)
    def _():
        pl.semaphore_signal(barrier, inc=1, device_id=(ves + 1, sec), device_id_type=MESH)

    for hop in hops:
        peer = lax.rem(sec + hop, n_sec)
        pl.semaphore_signal(barrier, inc=1, device_id=(ves, peer), device_id_type=MESH)

    def halo_copy(src, dst, slot, piece, to):
        return pltpu.make_async_remote_copy(
            src_ref=src,
            dst_ref=dst.at[slot],
            send_sem=send_sem.at[slot, piece],
            recv_sem=recv_sem.at[slot, piece],
            device_id=(to, sec),
            device_id_type=MESH,
        )

    def up_copy(piece):
        src, dst = ((tail01, recv01), (tail2, recv2))[piece]
        return halo_copy(src, dst, 0, piece, ves + 1)

    def down_copy(piece):
        src, dst = ((head01, recv01), (head2, recv2))[piece]
        return halo_copy(src, dst, 1, piece, ves - 1)

    def wall_copy(hop, kind):
        src, dst = (
            (coup_ref, coup_all.at[hop - 1]),
            (wgain_ref, gain_all.at[hop - 1]),
            (pick_all.at[sec], pick_all.at[sec]),
        )[kind]
        return pltpu.make_async_remote_copy(
            src_ref=src,
            dst_ref=dst,
            send_sem=wall_send.at[kind, hop - 1],
            recv_sem=wall_recv.at[kind, hop - 1],
            device_id=(ves, lax.rem(sec + hop, n_sec)),
            device_id_type=MESH,
        )

    @pl.when(jnp.logical_not(has_left))
    def _():
        recv01[0] = jnp.zeros(recv01.shape[1:], BF16)
        recv2[0] = jnp.zeros(recv2.shape[1:], BF16)

    @pl.when(jnp.logical_not(has_right))
    def _():
        recv01[1] = jnp.zeros(recv01.shape[1:], BF16)
        recv2[1] = jnp.zeros(recv2.shape[1:], BF16)

    low = lax.broadcasted_iota(jnp.int32, (num_coefs, tile), 1) < edge
    ana = ana_ref[...]

    def analyse(c):
        full = dot(ana, dens_ref[c])
        coef_ref[c] = full.astype(BF16)
        return full[:, :tile], full[:, count - tile :]

    head_0, tail_0 = analyse(0)
    head_1, tail_1 = analyse(1)
    tail01[...] = jnp.where(low, pltpu.roll(tail_0, edge, 1), tail_1).astype(BF16)
    head01[...] = jnp.where(low, head_0, pltpu.roll(head_1, edge, 1)).astype(BF16)

    pl.semaphore_wait(barrier, n_sec - 1 + has_left.astype(jnp.int32) + has_right.astype(jnp.int32))

    @pl.when(has_right)
    def _():
        up_copy(0).start()

    @pl.when(has_left)
    def _():
        down_copy(0).start()

    for hop in hops:
        wall_copy(hop, 0).start()
        wall_copy(hop, 1).start()

    head_2, tail_2 = analyse(2)
    low2 = low[:cut]
    tail2[...] = jnp.where(low2, pltpu.roll(tail_2, edge, 1)[:cut], tail_2[top:]).astype(BF16)
    head2[...] = jnp.where(low2, head_2[:cut], pltpu.roll(head_2, edge, 1)[top:]).astype(BF16)

    @pl.when(has_right)
    def _():
        up_copy(1).start()

    @pl.when(has_left)
    def _():
        down_copy(1).start()

    base = (ves * n_sec + sec) * count

    def placing(rows, first):
        row = lax.broadcasted_iota(jnp.int32, (rows, count), 0)
        ids = jnp.full((rows, count), -1, jnp.int32)
        for j in range(near_wall):
            ids = jnp.where(row == first + j, list_ref[j] - base, ids)
        hit = ids == lax.broadcasted_iota(jnp.int32, (rows, count), 1)
        return jnp.where(hit, 1.0, 0.0).astype(BF16)

    choose = placing(near_wall, 0)
    for c in range(comps):
        pick_all[sec, c] = dot(choose, coef_ref[c], 1, 1).astype(BF16)
    for hop in hops:
        wall_copy(hop, 2).start()

    shift = part_ref[...] - base
    weight = weight_ref[...]

    def mixing(rows, start):
        want = lax.broadcasted_iota(jnp.int32, (rows, count), 0) + start
        total = jnp.zeros((rows, count), F32)
        for k in range(shift.shape[0]):
            total = total + jnp.where(shift[k : k + 1, :] == want, weight[k : k + 1, :], 0.0)
        high = total.astype(BF16)
        return high, (total - high.astype(F32)).astype(BF16)

    own_high, own_low = mixing(count, 0)
    left_high, left_low = mixing(edge, count - edge - n_sec * count)
    right_high, right_low = mixing(edge, n_sec * count)
    none = jnp.zeros((edge, count), BF16)
    first_high = jnp.concatenate([left_high, none, right_high, none], axis=0)
    first_low = jnp.concatenate([left_low, none, right_low, none], axis=0)
    second_high = jnp.concatenate([none, left_high, none, right_high], axis=0)
    second_low = jnp.concatenate([none, left_low, none, right_low], axis=0)

    square = (num_coefs, num_coefs)
    diagonal = lax.broadcasted_iota(jnp.int32, square, 0) == lax.broadcasted_iota(
        jnp.int32, square, 1
    )
    gain = jnp.sum(jnp.where(diagonal, gain_ref[...], 0.0), axis=1, keepdims=True)

    syn = syn_ref[...]
    for c in range(comps):
        smooth = dot(syn, coef_ref[c], 0, 0).astype(BF16)
        mix_ref[c] = dot(smooth, own_high) + dot(smooth, own_low)

    for hop in hops:
        for kind in range(3):
            wall_copy(hop, kind).wait()
    coup = jnp.concatenate([coup_ref[...]] + [coup_all[hop - 1] for hop in hops], axis=1)
    wgain = jnp.concatenate([wgain_ref[...]] + [gain_all[hop - 1] for hop in hops], axis=1)
    place = placing(near_wall * n_sec, sec * near_wall)
    for c in range(comps):
        picked = jnp.concatenate([pick_all[s, c] for s in range(n_sec)], axis=0)
        dens = (dot(picked, coup, 0, 0) * wgain).astype(BF16)
        back = dot(coup, dens, 1, 1).astype(BF16)
        wall = dot(back, place, 0, 0).astype(BF16)
        scaled = (coef_ref[c].astype(F32) * gain).astype(BF16)
        out_ref[c] = dot(syn, scaled, 0, 0) + dot(syn, wall, 0, 0)

    def receive(piece):
        @pl.when(has_left)
        def _():
            up_copy(piece).wait_recv()

        @pl.when(has_right)
        def _():
            down_copy(piece).wait_recv()

    def finish(c, halo, high, lower):
        mixed = (mix_ref[c] + dot(halo, high) + dot(halo, lower)).astype(BF16)
        out_ref[c] = out_ref[c] + dot(near_ref[...], mixed, 0, 0)

    receive(0)
    both = jnp.concatenate([recv01[0], recv01[1]], axis=1)
    halo = dot(syn, both, 0, 0).astype(BF16)
    finish(0, halo, first_high, first_low)
    finish(1, halo, second_high, second_low)

    receive(1)
    for side in range(2):
        lanes = slice(side * tile, (side + 1) * tile)
        flat = recv2[side].astype(F32)
        halo2[:top, lanes] = flat[:top].astype(BF16)
        halo2[top:, lanes] = pltpu.roll(flat, edge, 1).astype(BF16)
    halo = dot(syn, halo2[...], 0, 0).astype(BF16)
    finish(2, halo, first_high, first_low)

    for piece in range(2):

        @pl.when(has_right)
        def _():
            up_copy(piece).wait_send()

        @pl.when(has_left)
        def _():
            down_copy(piece).wait_send()


def shards(
    n_ves,
    n_sec,
    density,
    analysis,
    synthesis,
    degree_gain,
    near_kernel,
    partners,
    pair_weight,
    wall_list,
    coupling,
    wall_gain,
):
    count, comps, num_points = density.shape
    num_coefs = analysis.shape[1]
    near_wall = wall_list.shape[0]
    panels, region_wall = coupling.shape
    tile = count // 2
    top = num_coefs // 2 // 16 * 16
    cut = num_coefs - top
    others = max(n_sec - 1, 1)
    vmem = pl.BlockSpec(memory_space=pltpu.VMEM)
    specs = [vmem] * 10
    specs[7] = pl.BlockSpec(memory_space=pltpu.SMEM)
    out = pl.pallas_call(
        functools.partial(step_kernel, n_ves, n_sec),
        name="vesicle_step",
        out_shape=OUT((comps, num_points, count)),
        in_specs=specs,
        out_specs=vmem,
        scratch_shapes=[
            pltpu.VMEM((comps, num_coefs, count), BF16),
            pltpu.VMEM((comps, num_points, count), F32),
            pltpu.VMEM((num_coefs, tile), BF16),
            pltpu.VMEM((cut, tile), BF16),
            pltpu.VMEM((num_coefs, tile), BF16),
            pltpu.VMEM((cut, tile), BF16),
            pltpu.VMEM((2, num_coefs, tile), BF16),
            pltpu.VMEM((2, cut, tile), BF16),
            pltpu.VMEM((num_coefs, 2 * tile), BF16),
            pltpu.VMEM((n_sec, comps, near_wall, num_coefs), BF16),
            pltpu.VMEM((others, region_wall, panels), BF16),
            pltpu.VMEM((others, 1, panels), F32),
            pltpu.SemaphoreType.DMA((2, 2)),
            pltpu.SemaphoreType.DMA((2, 2)),
            pltpu.SemaphoreType.DMA((3, others)),
            pltpu.SemaphoreType.DMA((3, others)),
        ],
        compiler_params=pltpu.CompilerParams(
            collective_id=0, has_side_effects=True, vmem_limit_bytes=32 * 1024 * 1024
        ),
    )(
        density.transpose(1, 2, 0),
        analysis.T,
        synthesis,
        degree_gain.reshape(1, num_coefs),
        near_kernel,
        partners.T,
        pair_weight.T,
        wall_list,
        coupling.T,
        wall_gain.reshape(1, panels),
    )
    return out.transpose(2, 0, 1)


def OUT(shape):
    return jax.ShapeDtypeStruct(shape, F32)


def solution(mesh):
    n_ves, n_sec = mesh.shape["ves"], mesh.shape["sec"]
    return jax.shard_map(
        functools.partial(shards, n_ves, n_sec),
        mesh=mesh,
        in_specs=(
            P(("ves", "sec"), None, None),
            P(),
            P(),
            P(),
            P(),
            P(("ves", "sec"), None),
            P(("ves", "sec"), None),
            P(("ves", "sec")),
            P(("ves", "sec"), None),
            P(("ves", "sec")),
        ),
        out_specs=P(("ves", "sec"), None, None),
        check_vma=False,
    )
```

time: 66.7 us -> 22.3 us (0.33)
  the two profiles are of different devices: /device:TPU:25 before, /device:TPU:0 now
where the time goes in v1:
time: 22.3 us; the launch traced here: 21.9 us
  Pallas kernels  12.4 us (56%)
  local copies, waits for them, and re-layouts  9.47 us (42%)
    pallas_call x1, Pallas kernels, shards(): pl.pallas_call(functools.partial(step_kernel, n_ves, n_sec), name='vesicl...  12.4 us
    unnamed x19, local copies, waits for them, and re-layouts  8.79 us
    reshape x1, local copies, waits for them, and re-layouts, shards(): degree_gain.reshape(1, num_coefs)  0.68 us

profile of v1, /device:TPU:0, one launch (start us, length us, event | category | flops | bytes accessed | tf_op | source)
XLA Modules:
  0.0 21.9 jit_solution(17105574989298130124)
XLA Ops:
  0.0 0.7 %reshape.6.gain_ref = f32[1,289]{1,0:T(1,128)S(1)} reshape(f32[289]{0:T(512)} %param.13) | data formatting | bytes 2312 | tf_op jit(solution)/shard_map/reshape | solution.py:316
  0.7 0.0 copy-start
  0.7 1.1 %copy-done = bf16[256,3,544]{0,2,1:T(8,128)(2,1)S(1)} copy-done((bf16[256,3,544]{0,2,1:T(8,128)(2,1)S(1)}, bf16[256,3,544]{0,2,1:T(8,128)(2,1)}, u32[]{:S(2)}) %copy-start) | copy-done | bytes 835608
  1.8 0.0 copy-start.1
  1.8 1.1 %copy-done.1 = bf16[544,544]{1,0:T(8,128)(2,1)S(1)} copy-done((bf16[544,544]{1,0:T(8,128)(2,1)S(1)}, bf16[544,544]{1,0:T(8,128)(2,1)}, u32[]{:S(2)}) %copy-start.1) | copy-done | bytes 591896
  2.9 0.0 copy-start.2
  2.9 1.0 %copy-done.2 = bf16[544,289]{0,1:T(8,128)(2,1)S(1)} copy-done((bf16[544,289]{0,1:T(8,128)(2,1)S(1)}, bf16[544,289]{0,1:T(8,128)(2,1)}, u32[]{:S(2)}) %copy-start.2) | copy-done | bytes 314456
  3.9 0.0 copy-start.3
  3.9 1.0 %copy-done.3 = bf16[289,544]{1,0:T(8,128)(2,1)S(1)} copy-done((bf16[289,544]{1,0:T(8,128)(2,1)S(1)}, bf16[289,544]{1,0:T(8,128)(2,1)}, u32[]{:S(2)}) %copy-start.3) | copy-done | bytes 314456
  4.9 0.0 copy-start.4
  4.9 0.7 %copy-done.4 = bf16[128,32]{0,1:T(8,128)(2,1)S(1)} copy-done((bf16[128,32]{0,1:T(8,128)(2,1)S(1)}, bf16[128,32]{0,1:T(8,128)(2,1)}, u32[]{:S(2)}) %copy-start.4) | copy-done | bytes 8216
  5.6 0.0 copy-start.5
  5.6 0.7 %copy-done.5 = s32[256,4]{0,1:T(4,128)S(1)} copy-done((s32[256,4]{0,1:T(4,128)S(1)}, s32[256,4]{0,1:T(4,128)}, u32[]{:S(2)}) %copy-start.5) | copy-done | bytes 4120
  6.3 0.0 copy-start.6
  6.3 0.7 %copy-done.6 = f32[256,4]{0,1:T(4,128)S(1)} copy-done((f32[256,4]{0,1:T(4,128)S(1)}, f32[256,4]{0,1:T(4,128)}, u32[]{:S(2)}) %copy-start.6) | copy-done | bytes 4120
  7.0 0.0 copy-start.7
  7.0 0.7 %copy-done.7 = s32[16]{0:T(128)S(1)} copy-done((s32[16]{0:T(128)S(1)}, s32[16]{0:T(128)}, u32[]{:S(2)}) %copy-start.7) | copy-done | bytes 88
  7.6 0.0 copy-start.8
  7.6 0.7 %copy-done.8 = f32[128]{0:T(128)S(1)} copy-done((f32[128]{0:T(128)S(1)}, f32[128]{0:T(128)}, u32[]{:S(2)}) %copy-start.8) | copy-done | bytes 536
  8.3 12.4 %vesicle_step.1 = f32[3,544,256]{2,1,0:T(8,128)S(1)} custom-call(bf16[3,544,256]{2,1,0:T(8,128)(2,1)S(1)} %bitcast.8, bf16[289,544]{1,0:T(8,128)(2,1)S(1)} %bitcast.9, bf16[289,544]{1,0:T(8,128)(2,1)S(1)} %copy-done.3, f32[1,289]{1,0:T(1,128)S(1)} %reshape.6.gain_ref, bf16[544,544]{1,0:T(8,128)(2,1)S(1)} %copy-done.1, s32[4,256]{1,0:T(4,128)S(1)} %bitcast.11, ...), custom_call_target="tpu_custom_call" | custom-call | tf_op jit(solution)/shard_map/vesicle_step/pallas_call | solution.py:285
  20.7 1.2 %copy.12 = f32[256,3,544]{0,2,1:T(8,128)} copy(f32[256,3,544]{0,2,1:T(8,128)S(1)} %bitcast.7) | data formatting | bytes 3342336
Async XLA Ops:
  0.7 1.1 %copy-start = (bf16[256,3,544]{0,2,1:T(8,128)(2,1)S(1)}, bf16[256,3,544]{0,2,1:T(8,128)(2,1)}, u32[]{:S(2)}) copy-start(bf16[256,3,544]{0,2,1:T(8,128)(2,1)} %param.10) | copy-start | bytes 2506756
  1.8 1.1 %copy-start.1 = (bf16[544,544]{1,0:T(8,128)(2,1)S(1)}, bf16[544,544]{1,0:T(8,128)(2,1)}, u32[]{:S(2)}) copy-start(bf16[544,544]{1,0:T(8,128)(2,1)} %near_ref.1) | copy-start | bytes 1775620
  2.9 1.0 %copy-start.2 = (bf16[544,289]{0,1:T(8,128)(2,1)S(1)}, bf16[544,289]{0,1:T(8,128)(2,1)}, u32[]{:S(2)}) copy-start(bf16[544,289]{0,1:T(8,128)(2,1)} %param.11) | copy-start | bytes 943300
  3.9 1.0 %copy-start.3 = (bf16[289,544]{1,0:T(8,128)(2,1)S(1)}, bf16[289,544]{1,0:T(8,128)(2,1)}, u32[]{:S(2)}) copy-start(bf16[289,544]{1,0:T(8,128)(2,1)} %syn_ref.1) | copy-start | bytes 943300
  4.9 0.7 %copy-start.4 = (bf16[128,32]{0,1:T(8,128)(2,1)S(1)}, bf16[128,32]{0,1:T(8,128)(2,1)}, u32[]{:S(2)}) copy-start(bf16[128,32]{0,1:T(8,128)(2,1)} %param.18) | copy-start | bytes 24580
  5.6 0.7 %copy-start.5 = (s32[256,4]{0,1:T(4,128)S(1)}, s32[256,4]{0,1:T(4,128)}, u32[]{:S(2)}) copy-start(s32[256,4]{0,1:T(4,128)} %param.15) | copy-start | bytes 12292
  6.3 0.7 %copy-start.6 = (f32[256,4]{0,1:T(4,128)S(1)}, f32[256,4]{0,1:T(4,128)}, u32[]{:S(2)}) copy-start(f32[256,4]{0,1:T(4,128)} %param.16) | copy-start | bytes 12292
  7.0 0.7 %copy-start.7 = (s32[16]{0:T(128)S(1)}, s32[16]{0:T(128)}, u32[]{:S(2)}) copy-start(s32[16]{0:T(128)} %list_ref.1) | copy-start | bytes 196
  7.6 0.7 %copy-start.8 = (f32[128]{0:T(128)S(1)}, f32[128]{0:T(128)}, u32[]{:S(2)}) copy-start(f32[128]{0:T(128)} %param.19) | copy-start | bytes 1540

commit v2 on v1

--- a/solution.py
+++ b/solution.py
@@ -19,17 +19,29 @@
 def step_kernel(
     n_ves,
     n_sec,
+    dens_in,
+    ana_in,
+    syn_in,
+    gain_ref,
+    near_in,
+    part_in,
+    weight_in,
+    list_in,
+    coup_in,
+    wgain_in,
+    out_ref,
     dens_ref,
     ana_ref,
     syn_ref,
-    gain_ref,
     near_ref,
     part_ref,
     weight_ref,
     list_ref,
     coup_ref,
     wgain_ref,
-    out_ref,
+    syn_turned,
+    near_turned,
+    load_sem,
     coef_ref,
     mix_ref,
     tail01,
@@ -49,7 +61,7 @@
 ):
     ves = lax.axis_index("ves")
     sec = lax.axis_index("sec")
-    comps, num_points, count = dens_ref.shape
+    comps, _, count = dens_ref.shape
     num_coefs = ana_ref.shape[0]
     near_wall = list_ref.shape[0]
     edge = count // 4
@@ -60,6 +72,25 @@
     has_right = ves < n_ves - 1
     hops = range(1, n_sec)
 
+    pairs = [(ana_in, ana_ref)]
+    pairs += [(dens_in.at[c], dens_ref.at[c]) for c in range(comps)]
+    pairs += [
+        (list_in, list_ref),
+        (part_in, part_ref),
+        (weight_in, weight_ref),
+        (syn_in, syn_ref),
+        (coup_in, coup_ref),
+        (wgain_in, wgain_ref),
+        (near_in, near_ref),
+    ]
+    loads = [
+        pltpu.make_async_copy(src, dst, load_sem.at[i]) for i, (src, dst) in enumerate(pairs)
+    ]
+    for load in loads:
+        load.start()
+    load_ana, *load_dens = loads[: comps + 1]
+    load_list, load_part, load_weight, load_syn, load_coup, load_wgain, load_near = loads[comps + 1 :]
+
     barrier = pltpu.get_barrier_semaphore()
 
     @pl.when(has_left)
@@ -94,8 +125,8 @@
 
     def wall_copy(hop, kind):
         src, dst = (
-            (coup_ref, coup_all.at[hop - 1]),
-            (wgain_ref, gain_all.at[hop - 1]),
+            (coup_in, coup_all.at[hop - 1]),
+            (wgain_in, gain_all.at[hop - 1]),
             (pick_all.at[sec], pick_all.at[sec]),
         )[kind]
         return pltpu.make_async_remote_copy(
@@ -118,9 +149,11 @@
         recv2[1] = jnp.zeros(recv2.shape[1:], BF16)
 
     low = lax.broadcasted_iota(jnp.int32, (num_coefs, tile), 1) < edge
+    load_ana.wait()
     ana = ana_ref[...]
 
     def analyse(c):
+        load_dens[c].wait()
         full = dot(ana, dens_ref[c])
         coef_ref[c] = full.astype(BF16)
         return full[:, :tile], full[:, count - tile :]
@@ -167,12 +200,15 @@
         hit = ids == lax.broadcasted_iota(jnp.int32, (rows, count), 1)
         return jnp.where(hit, 1.0, 0.0).astype(BF16)
 
+    load_list.wait()
     choose = placing(near_wall, 0)
     for c in range(comps):
         pick_all[sec, c] = dot(choose, coef_ref[c], 1, 1).astype(BF16)
     for hop in hops:
         wall_copy(hop, 2).start()
 
+    load_part.wait()
+    load_weight.wait()
     shift = part_ref[...] - base
     weight = weight_ref[...]
 
@@ -197,16 +233,22 @@
     diagonal = lax.broadcasted_iota(jnp.int32, square, 0) == lax.broadcasted_iota(
         jnp.int32, square, 1
     )
-    gain = jnp.sum(jnp.where(diagonal, gain_ref[...], 0.0), axis=1, keepdims=True)
-
-    syn = syn_ref[...]
+    gain = jnp.sum(jnp.where(diagonal, gain_ref[...].reshape(1, num_coefs), 0.0), axis=1, keepdims=True)
+
+    load_syn.wait()
+    syn_turned[...] = syn_ref[...].T
+    load_near.wait()
+    near_turned[...] = near_ref[...].T
+    syn = syn_turned[...]
     for c in range(comps):
-        smooth = dot(syn, coef_ref[c], 0, 0).astype(BF16)
+        smooth = dot(syn, coef_ref[c]).astype(BF16)
         mix_ref[c] = dot(smooth, own_high) + dot(smooth, own_low)
 
     for hop in hops:
         for kind in range(3):
             wall_copy(hop, kind).wait()
+    load_coup.wait()
+    load_wgain.wait()
     coup = jnp.concatenate([coup_ref[...]] + [coup_all[hop - 1] for hop in hops], axis=1)
     wgain = jnp.concatenate([wgain_ref[...]] + [gain_all[hop - 1] for hop in hops], axis=1)
     place = placing(near_wall * n_sec, sec * near_wall)
@@ -216,7 +258,7 @@
         back = dot(coup, dens, 1, 1).astype(BF16)
         wall = dot(back, place, 0, 0).astype(BF16)
         scaled = (coef_ref[c].astype(F32) * gain).astype(BF16)
-        out_ref[c] = dot(syn, scaled, 0, 0) + dot(syn, wall, 0, 0)
+        out_ref[c] = dot(syn, scaled) + dot(syn, wall)
 
     def receive(piece):
         @pl.when(has_left)
@@ -229,11 +271,11 @@
 
     def finish(c, halo, high, lower):
         mixed = (mix_ref[c] + dot(halo, high) + dot(halo, lower)).astype(BF16)
-        out_ref[c] = out_ref[c] + dot(near_ref[...], mixed, 0, 0)
+        out_ref[c] = out_ref[c] + dot(near_turned[...], mixed)
 
     receive(0)
     both = jnp.concatenate([recv01[0], recv01[1]], axis=1)
-    halo = dot(syn, both, 0, 0).astype(BF16)
+    halo = dot(syn, both).astype(BF16)
     finish(0, halo, first_high, first_low)
     finish(1, halo, second_high, second_low)
 
@@ -243,7 +285,7 @@
         flat = recv2[side].astype(F32)
         halo2[:top, lanes] = flat[:top].astype(BF16)
         halo2[top:, lanes] = pltpu.roll(flat, edge, 1).astype(BF16)
-    halo = dot(syn, halo2[...], 0, 0).astype(BF16)
+    halo = dot(syn, halo2[...]).astype(BF16)
     finish(2, halo, first_high, first_low)
 
     for piece in range(2):
@@ -280,15 +322,27 @@
     cut = num_coefs - top
     others = max(n_sec - 1, 1)
     vmem = pl.BlockSpec(memory_space=pltpu.VMEM)
-    specs = [vmem] * 10
-    specs[7] = pl.BlockSpec(memory_space=pltpu.SMEM)
+    specs = [pl.BlockSpec(memory_space=pltpu.HBM)] * 10
+    specs[3] = vmem
     out = pl.pallas_call(
         functools.partial(step_kernel, n_ves, n_sec),
         name="vesicle_step",
-        out_shape=OUT((comps, num_points, count)),
+        out_shape=jax.ShapeDtypeStruct((comps, num_points, count), F32),
         in_specs=specs,
         out_specs=vmem,
         scratch_shapes=[
+            pltpu.VMEM((comps, num_points, count), BF16),
+            pltpu.VMEM((num_coefs, num_points), BF16),
+            pltpu.VMEM((num_coefs, num_points), BF16),
+            pltpu.VMEM((num_points, num_points), BF16),
+            pltpu.VMEM(partners.shape[::-1], jnp.int32),
+            pltpu.VMEM(partners.shape[::-1], F32),
+            pltpu.SMEM((near_wall,), jnp.int32),
+            pltpu.VMEM((region_wall, panels), BF16),
+            pltpu.VMEM((1, panels), F32),
+            pltpu.VMEM((num_points, num_coefs), BF16),
+            pltpu.VMEM((num_points, num_points), BF16),
+            pltpu.SemaphoreType.DMA((comps + 8,)),
             pltpu.VMEM((comps, num_coefs, count), BF16),
             pltpu.VMEM((comps, num_points, count), F32),
             pltpu.VMEM((num_coefs, tile), BF16),
@@ -310,22 +364,23 @@
             collective_id=0, has_side_effects=True, vmem_limit_bytes=32 * 1024 * 1024
         ),
     )(
-        density.transpose(1, 2, 0),
-        analysis.T,
-        synthesis,
-        degree_gain.reshape(1, num_coefs),
-        near_kernel,
-        partners.T,
-        pair_weight.T,
-        wall_list,
-        coupling.T,
-        wall_gain.reshape(1, panels),
+        *(
+            pltpu.with_memory_space_constraint(array, pltpu.HBM)
+            for array in (
+                density.transpose(1, 2, 0),
+                analysis.T,
+                synthesis,
+                degree_gain,
+                near_kernel,
+                partners.T,
+                pair_weight.T,
+                wall_list,
+                coupling.T,
+                wall_gain.reshape(1, panels),
+            )
+        )
     )
     return out.transpose(2, 0, 1)
-
-
-def OUT(shape):
-    return jax.ShapeDtypeStruct(shape, F32)
 
 
 def solution(mesh):

time: 22.3 us -> 14.6 us (0.65); the launches traced: 21.9 us -> 14.5 us
  local copies, waits for them, and re-layouts: 9.47 us -> 1.18 us
  Pallas kernels: 12.4 us -> 13.3 us
    unnamed x19 -> x1, local copies, waits for them, and re-layouts: 8.79 us -> 1.18 us
    pallas_call x1, Pallas kernels: 12.4 us -> 13.3 us  [shards(): pl.pallas_call(functools.partial(step_kernel, n_ves, n_sec), name='vesicl...]
    reshape x1 -> x0, local copies, waits for them, and re-layouts: 0.68 us -> none  [shards(): degree_gain.reshape(1, num_coefs)]
where the time goes in v2:
time: 14.6 us; the launch traced here: 14.5 us
  Pallas kernels  13.3 us (91%)
  local copies, waits for them, and re-layouts  1.18 us (8%)
    pallas_call x1, Pallas kernels, shards(): pl.pallas_call(functools.partial(step_kernel, n_ves, n_sec), name='vesicl...  13.3 us
    unnamed x1, local copies, waits for them, and re-layouts  1.18 us

profile of v2, /device:TPU:0, one launch (start us, length us, event | category | flops | bytes accessed | tf_op | source)
XLA Modules:
  0.0 14.5 jit_solution(15894067786131393437)
XLA Ops:
  0.0 13.3 %vesicle_step.1 = f32[3,544,256]{2,1,0:T(8,128)S(1)} custom-call(bf16[3,544,256]{2,1,0:T(8,128)(2,1)} %bitcast.8, bf16[289,544]{1,0:T(8,128)(2,1)} %bitcast.9, bf16[289,544]{1,0:T(8,128)(2,1)} %syn_in.1, f32[289]{0:T(512)} %gain_ref.1, bf16[544,544]{1,0:T(8,128)(2,1)} %near_in.1, s32[4,256]{1,0:T(4,128)} %bitcast.11, f32[4,256]{1,0:T(4,128)} %bitcast.12, ...), custom_call_target="tpu_custom_call" | custom-call | tf_op jit(solution)/shard_map/vesicle_step/pallas_call | solution.py:327
  13.3 1.2 %copy.12 = f32[256,3,544]{0,2,1:T(8,128)} copy(f32[256,3,544]{0,2,1:T(8,128)S(1)} %bitcast.7) | data formatting | bytes 3342336

commit v3 on v2

--- a/solution.py
+++ b/solution.py
@@ -40,17 +40,15 @@
     coup_ref,
     wgain_ref,
     syn_turned,
-    near_turned,
+    both_high,
+    both_low,
     load_sem,
     coef_ref,
     mix_ref,
-    tail01,
-    tail2,
-    head01,
-    head2,
-    recv01,
-    recv2,
-    halo2,
+    total_ref,
+    tail_ref,
+    head_ref,
+    recv_ref,
     pick_all,
     coup_all,
     gain_all,
@@ -66,7 +64,7 @@
     near_wall = list_ref.shape[0]
     edge = count // 4
     tile = 2 * edge
-    cut = recv2.shape[1]
+    cut = recv_ref.shape[2]
     top = num_coefs - cut
     has_left = ves > 0
     has_right = ves < n_ves - 1
@@ -105,23 +103,21 @@
         peer = lax.rem(sec + hop, n_sec)
         pl.semaphore_signal(barrier, inc=1, device_id=(ves, peer), device_id_type=MESH)
 
-    def halo_copy(src, dst, slot, piece, to):
+    def halo_copy(src, side, c, to):
         return pltpu.make_async_remote_copy(
-            src_ref=src,
-            dst_ref=dst.at[slot],
-            send_sem=send_sem.at[slot, piece],
-            recv_sem=recv_sem.at[slot, piece],
+            src_ref=src.at[c],
+            dst_ref=recv_ref.at[side, c],
+            send_sem=send_sem.at[side, c],
+            recv_sem=recv_sem.at[side, c],
             device_id=(to, sec),
             device_id_type=MESH,
         )
 
-    def up_copy(piece):
-        src, dst = ((tail01, recv01), (tail2, recv2))[piece]
-        return halo_copy(src, dst, 0, piece, ves + 1)
-
-    def down_copy(piece):
-        src, dst = ((head01, recv01), (head2, recv2))[piece]
-        return halo_copy(src, dst, 1, piece, ves - 1)
+    def up_copy(c):
+        return halo_copy(tail_ref, 0, c, ves + 1)
+
+    def down_copy(c):
+        return halo_copy(head_ref, 1, c, ves - 1)
 
     def wall_copy(hop, kind):
         src, dst = (
@@ -140,55 +136,39 @@
 
     @pl.when(jnp.logical_not(has_left))
     def _():
-        recv01[0] = jnp.zeros(recv01.shape[1:], BF16)
-        recv2[0] = jnp.zeros(recv2.shape[1:], BF16)
+        recv_ref[0] = jnp.zeros(recv_ref.shape[1:], BF16)
 
     @pl.when(jnp.logical_not(has_right))
     def _():
-        recv01[1] = jnp.zeros(recv01.shape[1:], BF16)
-        recv2[1] = jnp.zeros(recv2.shape[1:], BF16)
-
-    low = lax.broadcasted_iota(jnp.int32, (num_coefs, tile), 1) < edge
+        recv_ref[1] = jnp.zeros(recv_ref.shape[1:], BF16)
+
+    low = lax.broadcasted_iota(jnp.int32, (cut, tile), 1) < edge
     load_ana.wait()
     ana = ana_ref[...]
 
-    def analyse(c):
+    for c in range(comps):
         load_dens[c].wait()
         full = dot(ana, dens_ref[c])
         coef_ref[c] = full.astype(BF16)
-        return full[:, :tile], full[:, count - tile :]
-
-    head_0, tail_0 = analyse(0)
-    head_1, tail_1 = analyse(1)
-    tail01[...] = jnp.where(low, pltpu.roll(tail_0, edge, 1), tail_1).astype(BF16)
-    head01[...] = jnp.where(low, head_0, pltpu.roll(head_1, edge, 1)).astype(BF16)
-
-    pl.semaphore_wait(barrier, n_sec - 1 + has_left.astype(jnp.int32) + has_right.astype(jnp.int32))
-
-    @pl.when(has_right)
-    def _():
-        up_copy(0).start()
-
-    @pl.when(has_left)
-    def _():
-        down_copy(0).start()
+        head = full[:, :tile]
+        tail = full[:, count - tile :]
+        tail_ref[c] = jnp.where(low, pltpu.roll(tail, edge, 1)[:cut], tail[top:]).astype(BF16)
+        head_ref[c] = jnp.where(low, head[:cut], pltpu.roll(head, edge, 1)[top:]).astype(BF16)
+        if c == 0:
+            sides = has_left.astype(jnp.int32) + has_right.astype(jnp.int32)
+            pl.semaphore_wait(barrier, n_sec - 1 + sides)
+
+        @pl.when(has_right)
+        def _():
+            up_copy(c).start()
+
+        @pl.when(has_left)
+        def _():
+            down_copy(c).start()
 
     for hop in hops:
         wall_copy(hop, 0).start()
         wall_copy(hop, 1).start()
-
-    head_2, tail_2 = analyse(2)
-    low2 = low[:cut]
-    tail2[...] = jnp.where(low2, pltpu.roll(tail_2, edge, 1)[:cut], tail_2[top:]).astype(BF16)
-    head2[...] = jnp.where(low2, head_2[:cut], pltpu.roll(head_2, edge, 1)[top:]).astype(BF16)
-
-    @pl.when(has_right)
-    def _():
-        up_copy(1).start()
-
-    @pl.when(has_left)
-    def _():
-        down_copy(1).start()
 
     base = (ves * n_sec + sec) * count
 
@@ -235,14 +215,16 @@
     )
     gain = jnp.sum(jnp.where(diagonal, gain_ref[...].reshape(1, num_coefs), 0.0), axis=1, keepdims=True)
 
+    for c in range(comps):
+        mix_ref[c] = dot(coef_ref[c], own_high) + dot(coef_ref[c], own_low)
+
     load_syn.wait()
     syn_turned[...] = syn_ref[...].T
+    syn = syn_turned[...]
     load_near.wait()
-    near_turned[...] = near_ref[...].T
-    syn = syn_turned[...]
-    for c in range(comps):
-        smooth = dot(syn, coef_ref[c]).astype(BF16)
-        mix_ref[c] = dot(smooth, own_high) + dot(smooth, own_low)
+    both = dot(near_ref[...].T, syn)
+    both_high[...] = both.astype(BF16)
+    both_low[...] = (both - both_high[...].astype(F32)).astype(BF16)
 
     for hop in hops:
         for kind in range(3):
@@ -256,47 +238,38 @@
         picked = jnp.concatenate([pick_all[s, c] for s in range(n_sec)], axis=0)
         dens = (dot(picked, coup, 0, 0) * wgain).astype(BF16)
         back = dot(coup, dens, 1, 1).astype(BF16)
-        wall = dot(back, place, 0, 0).astype(BF16)
+        wall = dot(back, place, 0, 0)
         scaled = (coef_ref[c].astype(F32) * gain).astype(BF16)
-        out_ref[c] = dot(syn, scaled) + dot(syn, wall)
-
-    def receive(piece):
+        out_ref[c] = dot(syn, scaled) + dot(syn, wall.astype(BF16))
+
+    def receive(c):
         @pl.when(has_left)
         def _():
-            up_copy(piece).wait_recv()
+            up_copy(c).wait_recv()
 
         @pl.when(has_right)
         def _():
-            down_copy(piece).wait_recv()
-
-    def finish(c, halo, high, lower):
-        mixed = (mix_ref[c] + dot(halo, high) + dot(halo, lower)).astype(BF16)
-        out_ref[c] = out_ref[c] + dot(near_turned[...], mixed)
-
-    receive(0)
-    both = jnp.concatenate([recv01[0], recv01[1]], axis=1)
-    halo = dot(syn, both).astype(BF16)
-    finish(0, halo, first_high, first_low)
-    finish(1, halo, second_high, second_low)
-
-    receive(1)
-    for side in range(2):
-        lanes = slice(side * tile, (side + 1) * tile)
-        flat = recv2[side].astype(F32)
-        halo2[:top, lanes] = flat[:top].astype(BF16)
-        halo2[top:, lanes] = pltpu.roll(flat, edge, 1).astype(BF16)
-    halo = dot(syn, halo2[...]).astype(BF16)
-    finish(2, halo, first_high, first_low)
-
-    for piece in range(2):
+            down_copy(c).wait_recv()
+
+    for c in range(comps):
+        receive(c)
+        halo = jnp.concatenate([recv_ref[0, c], recv_ref[1, c]], axis=1)
+        first = dot(halo[:top], first_high) + dot(halo[:top], first_low)
+        second = dot(halo, second_high) + dot(halo, second_low)
+        total_ref[:top] = (mix_ref[c, :top] + first).astype(BF16)
+        total_ref[top:] = (mix_ref[c, top:] + second).astype(BF16)
+        total = total_ref[...]
+        out_ref[c] = out_ref[c] + (dot(both_high[...], total) + dot(both_low[...], total))
+
+    for c in range(comps):
 
         @pl.when(has_right)
         def _():
-            up_copy(piece).wait_send()
+            up_copy(c).wait_send()
 
         @pl.when(has_left)
         def _():
-            down_copy(piece).wait_send()
+            down_copy(c).wait_send()
 
 
 def shards(
@@ -341,22 +314,20 @@
             pltpu.VMEM((region_wall, panels), BF16),
             pltpu.VMEM((1, panels), F32),
             pltpu.VMEM((num_points, num_coefs), BF16),
-            pltpu.VMEM((num_points, num_points), BF16),
+            pltpu.VMEM((num_points, num_coefs), BF16),
+            pltpu.VMEM((num_points, num_coefs), BF16),
             pltpu.SemaphoreType.DMA((comps + 8,)),
             pltpu.VMEM((comps, num_coefs, count), BF16),
-            pltpu.VMEM((comps, num_points, count), F32),
-            pltpu.VMEM((num_coefs, tile), BF16),
-            pltpu.VMEM((cut, tile), BF16),
-            pltpu.VMEM((num_coefs, tile), BF16),
-            pltpu.VMEM((cut, tile), BF16),
-            pltpu.VMEM((2, num_coefs, tile), BF16),
-            pltpu.VMEM((2, cut, tile), BF16),
-            pltpu.VMEM((num_coefs, 2 * tile), BF16),
+            pltpu.VMEM((comps, num_coefs, count), F32),
+            pltpu.VMEM((num_coefs, count), BF16),
+            pltpu.VMEM((comps, cut, tile), BF16),
+            pltpu.VMEM((comps, cut, tile), BF16),
+            pltpu.VMEM((2, comps, cut, tile), BF16),
             pltpu.VMEM((n_sec, comps, near_wall, num_coefs), BF16),
             pltpu.VMEM((others, region_wall, panels), BF16),
             pltpu.VMEM((others, 1, panels), F32),
-            pltpu.SemaphoreType.DMA((2, 2)),
-            pltpu.SemaphoreType.DMA((2, 2)),
+            pltpu.SemaphoreType.DMA((2, comps)),
+            pltpu.SemaphoreType.DMA((2, comps)),
             pltpu.SemaphoreType.DMA((3, others)),
             pltpu.SemaphoreType.DMA((3, others)),
         ],

time: 14.6 us -> 13.8 us (0.945)
  Pallas kernels: 13.3 us -> 12.5 us
    pallas_call x1, Pallas kernels: 13.3 us -> 12.5 us  [shards(): pl.pallas_call(functools.partial(step_kernel, n_ves, n_sec), name='vesicl...]
where the time goes in v3:
time: 13.8 us; the launch traced here: 13.6 us
  Pallas kernels  12.5 us (91%)
  local copies, waits for them, and re-layouts  1.18 us (9%)
    pallas_call x1, Pallas kernels, shards(): pl.pallas_call(functools.partial(step_kernel, n_ves, n_sec), name='vesicl...  12.5 us
    unnamed x1, local copies, waits for them, and re-layouts  1.18 us

profile of v3, /device:TPU:0, one launch (start us, length us, event | category | flops | bytes accessed | tf_op | source)
XLA Modules:
  0.0 13.6 jit_solution(12388681246515791535)
XLA Ops:
  0.0 12.5 %vesicle_step.1 = f32[3,544,256]{2,1,0:T(8,128)S(1)} custom-call(bf16[3,544,256]{2,1,0:T(8,128)(2,1)} %bitcast.8, bf16[289,544]{1,0:T(8,128)(2,1)} %bitcast.9, bf16[289,544]{1,0:T(8,128)(2,1)} %syn_in.1, f32[289]{0:T(512)} %gain_ref.1, bf16[544,544]{1,0:T(8,128)(2,1)} %near_in.1, s32[4,256]{1,0:T(4,128)} %bitcast.11, f32[4,256]{1,0:T(4,128)} %bitcast.12, ...), custom_call_target="tpu_custom_call" | custom-call | tf_op jit(solution)/shard_map/vesicle_step/pallas_call | solution.py:300
  12.5 1.2 %copy.12 = f32[256,3,544]{0,2,1:T(8,128)} copy(f32[256,3,544]{0,2,1:T(8,128)S(1)} %bitcast.7) | data formatting | bytes 3342336

commit v4 on v3

--- a/solution.py
+++ b/solution.py
@@ -40,8 +40,7 @@
     coup_ref,
     wgain_ref,
     syn_turned,
-    both_high,
-    both_low,
+    both_ref,
     load_sem,
     coef_ref,
     mix_ref,
@@ -70,6 +69,20 @@
     has_right = ves < n_ves - 1
     hops = range(1, n_sec)
 
+    barrier = pltpu.get_barrier_semaphore()
+
+    @pl.when(has_left)
+    def _():
+        pl.semaphore_signal(barrier, inc=1, device_id=(ves - 1, sec), device_id_type=MESH)
+
+    @pl.when(has_right)
+    def _():
+        pl.semaphore_signal(barrier, inc=1, device_id=(ves + 1, sec), device_id_type=MESH)
+
+    for hop in hops:
+        peer = lax.rem(sec + hop, n_sec)
+        pl.semaphore_signal(barrier, inc=1, device_id=(ves, peer), device_id_type=MESH)
+
     pairs = [(ana_in, ana_ref)]
     pairs += [(dens_in.at[c], dens_ref.at[c]) for c in range(comps)]
     pairs += [
@@ -89,20 +102,6 @@
     load_ana, *load_dens = loads[: comps + 1]
     load_list, load_part, load_weight, load_syn, load_coup, load_wgain, load_near = loads[comps + 1 :]
 
-    barrier = pltpu.get_barrier_semaphore()
-
-    @pl.when(has_left)
-    def _():
-        pl.semaphore_signal(barrier, inc=1, device_id=(ves - 1, sec), device_id_type=MESH)
-
-    @pl.when(has_right)
-    def _():
-        pl.semaphore_signal(barrier, inc=1, device_id=(ves + 1, sec), device_id_type=MESH)
-
-    for hop in hops:
-        peer = lax.rem(sec + hop, n_sec)
-        pl.semaphore_signal(barrier, inc=1, device_id=(ves, peer), device_id_type=MESH)
-
     def halo_copy(src, side, c, to):
         return pltpu.make_async_remote_copy(
             src_ref=src.at[c],
@@ -197,17 +196,14 @@
         total = jnp.zeros((rows, count), F32)
         for k in range(shift.shape[0]):
             total = total + jnp.where(shift[k : k + 1, :] == want, weight[k : k + 1, :], 0.0)
-        high = total.astype(BF16)
-        return high, (total - high.astype(F32)).astype(BF16)
-
-    own_high, own_low = mixing(count, 0)
-    left_high, left_low = mixing(edge, count - edge - n_sec * count)
-    right_high, right_low = mixing(edge, n_sec * count)
+        return total.astype(BF16)
+
+    own_mix = mixing(count, 0)
+    left_mix = mixing(edge, count - edge - n_sec * count)
+    right_mix = mixing(edge, n_sec * count)
     none = jnp.zeros((edge, count), BF16)
-    first_high = jnp.concatenate([left_high, none, right_high, none], axis=0)
-    first_low = jnp.concatenate([left_low, none, right_low, none], axis=0)
-    second_high = jnp.concatenate([none, left_high, none, right_high], axis=0)
-    second_low = jnp.concatenate([none, left_low, none, right_low], axis=0)
+    first_mix = jnp.concatenate([left_mix, none, right_mix, none], axis=0)
+    second_mix = jnp.concatenate([none, left_mix, none, right_mix], axis=0)
 
     square = (num_coefs, num_coefs)
     diagonal = lax.broadcasted_iota(jnp.int32, square, 0) == lax.broadcasted_iota(
@@ -216,15 +212,13 @@
     gain = jnp.sum(jnp.where(diagonal, gain_ref[...].reshape(1, num_coefs), 0.0), axis=1, keepdims=True)
 
     for c in range(comps):
-        mix_ref[c] = dot(coef_ref[c], own_high) + dot(coef_ref[c], own_low)
+        mix_ref[c] = dot(coef_ref[c], own_mix)
 
     load_syn.wait()
     syn_turned[...] = syn_ref[...].T
     syn = syn_turned[...]
     load_near.wait()
-    both = dot(near_ref[...].T, syn)
-    both_high[...] = both.astype(BF16)
-    both_low[...] = (both - both_high[...].astype(F32)).astype(BF16)
+    both_ref[...] = dot(near_ref[...].T, syn).astype(BF16)
 
     for hop in hops:
         for kind in range(3):
@@ -239,8 +233,8 @@
         dens = (dot(picked, coup, 0, 0) * wgain).astype(BF16)
         back = dot(coup, dens, 1, 1).astype(BF16)
         wall = dot(back, place, 0, 0)
-        scaled = (coef_ref[c].astype(F32) * gain).astype(BF16)
-        out_ref[c] = dot(syn, scaled) + dot(syn, wall.astype(BF16))
+        scaled = coef_ref[c].astype(F32) * gain
+        out_ref[c] = dot(syn, (scaled + wall).astype(BF16))
 
     def receive(c):
         @pl.when(has_left)
@@ -254,12 +248,12 @@
     for c in range(comps):
         receive(c)
         halo = jnp.concatenate([recv_ref[0, c], recv_ref[1, c]], axis=1)
-        first = dot(halo[:top], first_high) + dot(halo[:top], first_low)
-        second = dot(halo, second_high) + dot(halo, second_low)
+        first = dot(halo[:top], first_mix)
+        second = dot(halo, second_mix)
         total_ref[:top] = (mix_ref[c, :top] + first).astype(BF16)
         total_ref[top:] = (mix_ref[c, top:] + second).astype(BF16)
         total = total_ref[...]
-        out_ref[c] = out_ref[c] + (dot(both_high[...], total) + dot(both_low[...], total))
+        out_ref[c] = out_ref[c] + dot(both_ref[...], total)
 
     for c in range(comps):
 
@@ -315,7 +309,6 @@
             pltpu.VMEM((1, panels), F32),
             pltpu.VMEM((num_points, num_coefs), BF16),
             pltpu.VMEM((num_points, num_coefs), BF16),
-            pltpu.VMEM((num_points, num_coefs), BF16),
             pltpu.SemaphoreType.DMA((comps + 8,)),
             pltpu.VMEM((comps, num_coefs, count), BF16),
             pltpu.VMEM((comps, num_coefs, count), F32),

time: 13.8 us -> 13.1 us (0.949)
  Pallas kernels: 12.5 us -> 11.7 us
    pallas_call x1, Pallas kernels: 12.5 us -> 11.7 us  [shards(): pl.pallas_call(functools.partial(step_kernel, n_ves, n_sec), name='vesicl...]
where the time goes in v4:
time: 13.1 us; the launch traced here: 12.9 us
  Pallas kernels  11.7 us (89%)
  local copies, waits for them, and re-layouts  1.18 us (9%)
    pallas_call x1, Pallas kernels, shards(): pl.pallas_call(functools.partial(step_kernel, n_ves, n_sec), name='vesicl...  11.7 us
    unnamed x1, local copies, waits for them, and re-layouts  1.18 us

profile of v4, /device:TPU:0, one launch (start us, length us, event | category | flops | bytes accessed | tf_op | source)
XLA Modules:
  0.0 12.9 jit_solution(15928298826781295695)
XLA Ops:
  0.0 11.7 %vesicle_step.1 = f32[3,544,256]{2,1,0:T(8,128)S(1)} custom-call(bf16[3,544,256]{2,1,0:T(8,128)(2,1)} %bitcast.8, bf16[289,544]{1,0:T(8,128)(2,1)} %bitcast.9, bf16[289,544]{1,0:T(8,128)(2,1)} %syn_in.1, f32[289]{0:T(512)} %gain_ref.1, bf16[544,544]{1,0:T(8,128)(2,1)} %near_in.1, s32[4,256]{1,0:T(4,128)} %bitcast.11, f32[4,256]{1,0:T(4,128)} %bitcast.12, ...), custom_call_target="tpu_custom_call" | custom-call | tf_op jit(solution)/shard_map/vesicle_step/pallas_call | solution.py:294
  11.7 1.2 %copy.12 = f32[256,3,544]{0,2,1:T(8,128)} copy(f32[256,3,544]{0,2,1:T(8,128)S(1)} %bitcast.7) | data formatting | bytes 3342336

commit v5 on v4

--- a/solution.py
+++ b/solution.py
@@ -89,18 +89,18 @@
         (list_in, list_ref),
         (part_in, part_ref),
         (weight_in, weight_ref),
-        (syn_in, syn_ref),
         (coup_in, coup_ref),
         (wgain_in, wgain_ref),
+        (syn_in, syn_ref),
         (near_in, near_ref),
     ]
     loads = [
         pltpu.make_async_copy(src, dst, load_sem.at[i]) for i, (src, dst) in enumerate(pairs)
     ]
-    for load in loads:
+    for load in loads[:-2]:
         load.start()
     load_ana, *load_dens = loads[: comps + 1]
-    load_list, load_part, load_weight, load_syn, load_coup, load_wgain, load_near = loads[comps + 1 :]
+    load_list, load_part, load_weight, load_coup, load_wgain, load_syn, load_near = loads[comps + 1 :]
 
     def halo_copy(src, side, c, to):
         return pltpu.make_async_remote_copy(
@@ -164,6 +164,10 @@
         @pl.when(has_left)
         def _():
             down_copy(c).start()
+
+        if c == 0:
+            load_syn.start()
+            load_near.start()
 
     for hop in hops:
         wall_copy(hop, 0).start()

time: 13.1 us -> 13.1 us (level)
  no operation moved by 1% of the time
where the time goes in v5:
time: 13.1 us; the launch traced here: 12.9 us
  Pallas kernels  11.7 us (89%)
  local copies, waits for them, and re-layouts  1.18 us (9%)
    pallas_call x1, Pallas kernels, shards(): pl.pallas_call(functools.partial(step_kernel, n_ves, n_sec), name='vesicl...  11.7 us
    unnamed x1, local copies, waits for them, and re-layouts  1.18 us

profile of v5, /device:TPU:0, one launch (start us, length us, event | category | flops | bytes accessed | tf_op | source)
XLA Modules:
  0.0 12.9 jit_solution(7051003170579590429)
XLA Ops:
  0.0 11.7 %vesicle_step.1 = f32[3,544,256]{2,1,0:T(8,128)S(1)} custom-call(bf16[3,544,256]{2,1,0:T(8,128)(2,1)} %bitcast.8, bf16[289,544]{1,0:T(8,128)(2,1)} %bitcast.9, bf16[289,544]{1,0:T(8,128)(2,1)} %syn_in.1, f32[289]{0:T(512)} %gain_ref.1, bf16[544,544]{1,0:T(8,128)(2,1)} %near_in.1, s32[4,256]{1,0:T(4,128)} %bitcast.11, f32[4,256]{1,0:T(4,128)} %bitcast.12, ...), custom_call_target="tpu_custom_call" | custom-call | tf_op jit(solution)/shard_map/vesicle_step/pallas_call | solution.py:298
  11.7 1.2 %copy.12 = f32[256,3,544]{0,2,1:T(8,128)} copy(f32[256,3,544]{0,2,1:T(8,128)S(1)} %bitcast.7) | data formatting | bytes 3342336
